TPU v7x, 512 devices: a whole 4x4x16 slice. The times are simulated.
512 devices in a mesh: group: 64 (over z, y_hi, core), tp: 8 (over x, y_lo).
Axes of the slice: x: 4, y: 4 (y_hi: 2, y_lo: 2; y = y_hi * 2 + y_lo), z: 16, core: 2. Of those that a mesh axis runs over, the one named last changes fastest.
Arguments:
- queries: bfloat16 [4096, 2048], P('group', 'tp'), may hold values from -22 to 22
- new_kv: bfloat16 [4096, 1024], P('group', 'tp'), may hold values from -6 to 6
- local_cache: bfloat16 [16384, 1024], P('group', 'tp'), may hold values from -6 to 6
- remote_pool: bfloat16 [32768, 1024], P('group', 'tp'), may hold values from -6 to 6
- page_index: int32 [64, 64], P('group'), may hold values from 0 to 63, each once within a row
- lengths: int32 [64], P('group'), may hold values from 256 to 768, as said below
- sinks: float32 [32], P('tp'), may hold values from 4 to 8
- out_weight: bfloat16 [2048, 2880], P('tp'), may hold values from -0.125 to 0.125
- residual: bfloat16 [4096, 2880], P('group', 'tp'), may hold values from -6 to 6
- norm_gain: float32 [2880], replicated, may hold values from 0.5 to 2
- routes: int32 [4096, 4], P('group'), may hold values from 0 to 31, all different within a row; in each aligned block of 64 rows (0 to 63, 64 to 127, ...) at most 10 rows name the same one
- route_weights: float32 [4096, 4], P('group'), may hold values from 0.1 to 1
- expert_gate: bfloat16 [64, 2880, 1440], P('group', None, 'tp'), may hold values from -0.109375 to 0.109375
- expert_up: bfloat16 [64, 2880, 1440], P('group', None, 'tp'), may hold values from -0.109375 to 0.109375
- expert_down: bfloat16 [64, 1440, 2880], P('group', None, 'tp'), may hold values from -0.109375 to 0.109375
Outputs:
- layer_out: bfloat16 [4096, 2880], P('group', 'tp')
Inputs may be any that keep to these rules, and one draw needn't show every extreme that they name: `lengths`: every request has at least 256 cached positions; some request has exactly 256, some exactly 768. `routes`: within the rows of one request no expert is named by more than 10 rows. `page_index`: each row is a permutation.
All inputs are finite; a program needn't handle non-finite values.
Results may differ from a plain program's by a relative error of at most 0.013.
Values may be sent and summed in bfloat16 or wider, within the bound.
A program may use at most 64 MiB of HBM per device.

v0:
```python
import jax
import jax.numpy as jnp
from jax import lax
from jax.sharding import PartitionSpec as P

HEAD = 64
THETA = 150000.0
ALPHA = 1.702
EPSILON = 1e-05


def rotate(values, positions):
    half_dim = values.shape[-1] // 2
    inverse = THETA ** (-2.0 * jnp.arange(half_dim, dtype=jnp.float32) / values.shape[-1])
    angles = positions[:, None, None] * inverse[None, None, :]
    cosine = jnp.cos(angles)
    sine_part = jnp.sin(angles)
    first_part = values[..., :half_dim]
    second_part = values[..., half_dim:]
    return jnp.concatenate(
        [
            first_part * cosine - second_part * sine_part,
            second_part * cosine + first_part * sine_part,
        ],
        axis=-1,
    )


def attend(query_rows, kv_rows, cache_kv, cache_valid, sinks, length):
    block_len = query_rows.shape[0]
    kv_heads = kv_rows.shape[1] // (2 * HEAD)
    query_heads = query_rows.shape[1] // HEAD
    group_size = query_heads // kv_heads
    positions = (length + jnp.arange(block_len, dtype=jnp.int32)).astype(jnp.float32)
    query_rot = rotate(
        query_rows.astype(jnp.float32).reshape(block_len, query_heads, HEAD), positions
    ).astype(jnp.bfloat16)
    kv_parts = kv_rows.reshape(block_len, kv_heads, 2, HEAD)
    key_rot = rotate(kv_parts[:, :, 0].astype(jnp.float32), positions).astype(jnp.bfloat16)
    cache_parts = cache_kv.reshape(cache_kv.shape[0], kv_heads, 2, HEAD)
    all_keys = jnp.concatenate([cache_parts[:, :, 0], key_rot], axis=0)
    all_values = jnp.concatenate([cache_parts[:, :, 1], kv_parts[:, :, 1]], axis=0)
    token_order = jnp.arange(block_len, dtype=jnp.int32)
    causal = token_order[None, :] <= token_order[:, None]
    allowed = jnp.concatenate(
        [jnp.broadcast_to(cache_valid[None, :], (block_len, cache_valid.shape[0])), causal], axis=1
    )
    row_allowed = jnp.repeat(allowed, group_size, axis=0)
    score_scale = HEAD ** (-0.5)
    query_block = query_rot.reshape(block_len * group_size, HEAD)
    scores = (
        jnp.dot(query_block, all_keys[:, 0].T, preferred_element_type=jnp.float32) * score_scale
    )
    scores = jnp.where(row_allowed, scores, -jnp.inf)
    sink_rows = jnp.tile(sinks, block_len)
    row_max = jnp.maximum(jnp.max(scores, axis=1), sink_rows)
    weights = jnp.exp(scores - row_max[:, None])
    denominator = jnp.sum(weights, axis=1) + jnp.exp(sink_rows - row_max)
    blended = (
        jnp.dot(weights.astype(jnp.bfloat16), all_values[:, 0], preferred_element_type=jnp.float32)
        / denominator[:, None]
    )
    outputs = blended.astype(jnp.bfloat16).reshape(block_len, group_size * HEAD)
    return outputs


def on_device(
    queries,
    new_kv,
    local_cache,
    remote_pool,
    page_index,
    lengths,
    sinks,
    out_weight,
    residual,
    norm_gain,
    routes,
    route_weights,
    expert_gate,
    expert_up,
    expert_down,
):
    groups = lax.axis_size("group")
    lane_count = remote_pool.shape[1]
    local_len = local_cache.shape[0]
    fetched = lax.all_to_all(
        remote_pool.reshape(groups, -1, lane_count),
        "group",
        split_axis=0,
        concat_axis=0,
        tiled=True,
    )
    page_len = fetched.shape[1]
    length = lengths[0]
    offsets = jnp.arange(page_len, dtype=jnp.int32)
    remote_pos = local_len + page_index[0][:, None] * page_len + offsets[None, :]
    cache_valid = jnp.concatenate(
        [jnp.ones((local_len,), jnp.bool_), (remote_pos < length).reshape(-1)]
    )
    cache_kv = jnp.concatenate([local_cache, fetched.reshape(-1, lane_count)], axis=0)
    attended = attend(queries, new_kv, cache_kv, cache_valid, sinks, length)
    width = residual.shape[1]
    start = lax.axis_index("tp") * width
    own_gain = lax.dynamic_slice_in_dim(norm_gain, start, width, 0)
    partial_sum = jnp.dot(attended, out_weight, preferred_element_type=jnp.float32)
    own_cols = lax.dynamic_slice_in_dim(partial_sum, start, width, 1) + residual.astype(jnp.float32)
    partial_sum = lax.dynamic_update_slice_in_dim(partial_sum, own_cols, start, 1)
    hidden_state = lax.psum(partial_sum, "tp")
    mean_square = jnp.mean(hidden_state * hidden_state, axis=1, keepdims=True)
    own_state = lax.dynamic_slice_in_dim(hidden_state, start, width, 1)
    normed_own = (own_state * lax.rsqrt(mean_square + EPSILON) * own_gain).astype(jnp.bfloat16)
    block_len = normed_own.shape[0]
    top_count = routes.shape[1]
    experts = groups // 2
    capacity = 5 * block_len * top_count // (4 * experts)
    member = jnp.any(
        routes[:, :, None] == jnp.arange(experts, dtype=jnp.int32)[None, None, :], axis=1
    ).astype(jnp.int32)
    slot_rank = jnp.cumsum(member, axis=0) - member
    slot_hit = member[:, :, None] * (
        slot_rank[:, :, None] == jnp.arange(capacity, dtype=jnp.int32)[None, None, :]
    ).astype(jnp.int32)
    slot_token = jnp.sum(slot_hit * jnp.arange(block_len, dtype=jnp.int32)[:, None, None], axis=0)
    slot_valid = jnp.sum(slot_hit, axis=0)
    send_own = jnp.take(normed_own, slot_token.reshape(-1), axis=0) * slot_valid.reshape(
        -1, 1
    ).astype(jnp.bfloat16)
    hidden_part = expert_gate.shape[2]
    gate_and_up = jnp.concatenate([expert_gate[0], expert_up[0]], axis=1)
    outgoing = send_own
    feature_count = outgoing.shape[1]
    outgoing = outgoing.reshape(experts, 1, capacity, feature_count)
    outgoing = jnp.broadcast_to(outgoing, (experts, 2, capacity, feature_count)).reshape(
        groups, capacity, feature_count
    )
    whole = lax.all_gather(
        lax.all_to_all(outgoing, "group", split_axis=0, concat_axis=0, tiled=True),
        "tp",
        axis=2,
        tiled=True,
    )
    sources, slot_count, features = whole.shape
    flat_rows = whole.reshape(sources * slot_count, features)
    both = jnp.dot(flat_rows, gate_and_up, preferred_element_type=jnp.float32)
    gate_val = both[:, :hidden_part]
    up_val = both[:, hidden_part:]
    active = (gate_val * jax.nn.sigmoid(ALPHA * gate_val) * (up_val + 1.0)).astype(jnp.bfloat16)
    joined = lax.all_gather(active, "tp", axis=1, tiled=True)
    result = jnp.dot(joined, expert_down[0], preferred_element_type=jnp.float32).astype(
        jnp.bfloat16
    )
    returned = result.reshape(sources, slot_count, result.shape[1])
    arrived = lax.all_to_all(returned, "group", split_axis=0, concat_axis=0, tiled=True)
    halves = arrived.reshape(experts, 2, capacity, width).astype(jnp.float32)
    summed = (halves[:, 0] + halves[:, 1]).reshape(experts * capacity, width)
    rank_at = jnp.take_along_axis(slot_rank, routes, axis=1)
    picked = jnp.take(summed, (routes * capacity + rank_at).reshape(-1), axis=0).reshape(
        block_len, top_count, width
    )
    mixing = route_weights / jnp.sum(route_weights, axis=1, keepdims=True)
    moe_out = jnp.sum(mixing[:, :, None] * picked, axis=1)
    return (own_state + moe_out).astype(jnp.bfloat16)


def solution(mesh):
    return jax.shard_map(
        on_device,
        mesh=mesh,
        in_specs=(
            P("group", "tp"),
            P("group", "tp"),
            P("group", "tp"),
            P("group", "tp"),
            P("group", None),
            P("group"),
            P("tp"),
            P("tp", None),
            P("group", "tp"),
            P(),
            P("group", None),
            P("group", None),
            P("group", None, "tp"),
            P("group", None, "tp"),
            P("group", None, "tp"),
        ),
        out_specs=P("group", "tp"),
        check_vma=False,
    )
```

profile of v0, /device:TPU:2, one launch (start us, length us, event | category | flops | bytes accessed | tf_op | source)
XLA Modules:
  0.0 590.5 jit_solution(3634151493439080288)
XLA Ops:
  6.5 18.9 %all-to-all-start = ((bf16[64,8,128]{2,1,0:T(8,128)(2,1)}), bf16[64,8,128]{2,1,0:T(8,128)(2,1)S(1)}, u32[]{:S(2)}, u32[]{:S(2)}) async-start(bf16[64,8,128]{2,1,0:T(8,128)(2,1)} %bitcast.65), calls=%async_computation | async-start | bytes 262144 | tf_op jit(solution)/shard_map/all_to_all | solution.py:87
  26.2 0.9 reshape.390
  27.0 0.8 copy.147
  27.9 0.9 copy.144
  29.0 0.7 add_bitcast_fusion
  29.8 0.2 broadcast_in_dim.31
  30.1 0.3 reshape.377
  30.3 0.3 copy.148
  30.8 0.1 fusion.31
  31.2 0.8 dynamic_slice.11
  32.0 0.2 multiply_cosine_fusion
  32.2 0.2 subtract_convert_fusion
  32.4 11.6 %all-to-all-done = bf16[64,8,128]{2,1,0:T(8,128)(2,1)S(1)} async-done(((bf16[64,8,128]{2,1,0:T(8,128)(2,1)}), bf16[64,8,128]{2,1,0:T(8,128)(2,1)S(1)}, u32[]{:S(2)}, u32[]{:S(2)}) %all-to-all-start) | async-done | bytes 131104 | tf_op jit(solution)/shard_map/all_to_all | solution.py:87
  44.1 0.7 slice_maximum_fusion
  44.8 0.3 copy.146
  45.1 0.4 fusion.40
  45.5 0.2 fusion.8
  45.7 0.3 copy.149
  46.0 0.3 fusion.5
  46.6 0.6 fusion.41
  47.3 1.1 dynamic_update_slice.3
  48.4 0.9 copy-done.1
  49.4 0.4 select_reduce_fusion
  50.3 78.5 %all-reduce.3.cloned.1.call-done = f32[64,2880]{1,0:T(8,128)} async-done(((f32[64,2880]{1,0:T(8,128)}), f32[64,2880]{1,0:T(8,128)}) %all-reduce.3.cloned.1.call-update) | async-done | bytes 737296 | tf_op jit(solution)/shard_map/psum | solution.py:109
  128.8 1.3 multiply_reduce_fusion
  130.1 1.0 multiply_convert_fusion
  131.1 2.0 gather_fusion
  133.3 0.2 select_multiply_fusion
  133.6 59.9 %all_to_all.15 = bf16[64,10,360]{2,1,0:T(8,128)(2,1)S(1)} all-to-all(bf16[64,10,360]{2,1,0:T(8,128)(2,1)S(1)} %bitcast.58), channel_id=1, replica_groups=mesh['group'=64,'tp'=8] {'group'}, dimensions={0} | all-to-all | bytes 921600 | tf_op jit(solution)/shard_map/all_to_all | solution.py:138
  193.5 2.0 copy.165
  195.5 0.2 all-gather.6.cloned.1.call-start
  195.8 231.1 %all-gather.4.cloned.1.call-done = bf16[64,10,2880]{0,1,2:T(8,128)(2,1)} async-done(((bf16[64,10,360]{0,1,2:T(8,128)(2,1)}), bf16[64,10,2880]{0,1,2:T(8,128)(2,1)}) %all-gather.4.cloned.1.call-update) | async-done | bytes 3686416 | tf_op jit(solution)/shard_map/all_gather | solution.py:137
  426.8 17.0 %copy.166 = bf16[64,10,2880]{2,1,0:T(8,128)(2,1)} copy(bf16[64,10,2880]{0,1,2:T(8,128)(2,1)} %all-gather.4.cloned.1.call-done) | data formatting | bytes 7372800 | tf_op jit(solution)/shard_map/all_gather | solution.py:137
  443.8 7.9 %reshape.386 = bf16[640,2880]{1,0:T(8,128)(2,1)} reshape(bf16[64,10,2880]{2,1,0:T(8,128)(2,1)} %copy.166) | data formatting | bytes 7372800 | tf_op jit(solution)/shard_map/reshape | solution.py:144
  451.7 4.3 fusion
  456.0 0.9 fusion.14
  456.8 55.6 %all-gather.6.cloned.1.call-done = bf16[8,180,640]{2,1,0:T(8,128)(2,1)} async-done(((bf16[1,180,640]{2,1,0:T(8,128)(2,1)}), bf16[8,180,640]{2,1,0:T(8,128)(2,1)}) %all-gather.6.cloned.1.call-update) | async-done | bytes 1843216 | tf_op jit(solution)/shard_map/all_gather | solution.py:149
  512.5 1.7 reshape.421
  514.2 3.1 convolution_convert_fusion
  517.3 1.3 copy.167
  518.5 1.1 reshape.387
  519.6 16.0 %all-to-all-start.2 = ((bf16[64,10,360]{2,1,0:T(8,128)(2,1)}), bf16[64,10,360]{2,1,0:T(8,128)(2,1)S(1)}, u32[]{:S(2)}, u32[]{:S(2)}) async-start(bf16[64,10,360]{2,1,0:T(8,128)(2,1)} %reshape.387), calls=%async_computation.2 | async-start | bytes 1572864 | tf_op jit(solution)/shard_map/all_to_all | solution.py:154
  535.9 1.9 gather_fusion.2
  538.5 42.0 %all-to-all-done.2 = bf16[64,10,360]{2,1,0:T(8,128)(2,1)S(1)} async-done(((bf16[64,10,360]{2,1,0:T(8,128)(2,1)}), bf16[64,10,360]{2,1,0:T(8,128)(2,1)S(1)}, u32[]{:S(2)}, u32[]{:S(2)}) %all-to-all-start.2) | async-done | bytes 460832 | tf_op jit(solution)/shard_map/all_to_all | solution.py:154
  580.5 0.2 convert.22
  580.9 1.0 gather_fusion.1
  582.0 0.4 multiply_reduce_fusion.1
  582.4 1.6 add_convert_fusion.1
  (70 shorter events, 3.2 us)
Async XLA Ops:
  6.5 40.0 %copy-start = (bf16[256,2880]{0,1:T(8,128)(2,1)S(1)}, bf16[256,2880]{0,1:T(8,128)(2,1)}, u32[]{:S(2)}) copy-start(bf16[256,2880]{0,1:T(8,128)(2,1)} %param.22) | copy-start | bytes 4423684
  6.5 24.1 %copy-start.5 = (f32[4]{0:T(128)S(1)}, f32[4]{0:T(128)}, u32[]{:S(2)}) copy-start(f32[4]{0:T(128)} %param.21) | copy-start | bytes 52
  6.5 24.4 %copy-start.3 = (s32[64,4]{0,1:T(4,128)S(1)}, s32[64,4]{0,1:T(4,128)}, u32[]{:S(2)}) copy-start(s32[64,4]{0,1:T(4,128)} %param.25) | copy-start | bytes 3076
  6.5 37.4 %all-to-all-start = ((bf16[64,8,128]{2,1,0:T(8,128)(2,1)}), bf16[64,8,128]{2,1,0:T(8,128)(2,1)S(1)}, u32[]{:S(2)}, u32[]{:S(2)}) async-start(bf16[64,8,128]{2,1,0:T(8,128)(2,1)} %bitcast.65), calls=%async_computation | async-start | bytes 262144 | tf_op jit(solution)/shard_map/all_to_all | solution.py:87
  25.4 103.4 %all-reduce.3.cloned.1.call-start = ((), (), s32[]{:S(2)}) async-start(), calls=%async_computation.3 | async-start | bytes 1507328 | tf_op jit(solution)/shard_map/psum | solution.py:109
  46.0 1.1 copy-start.2
  48.4 0.9 copy-start.1
  49.3 377.6 %all-gather.4.cloned.1.call-start = ((), (), s32[]{:S(2)}) async-start(), calls=%async_computation.4 | async-start | bytes 13271040 | tf_op jit(solution)/shard_map/all_gather | solution.py:137
  195.5 316.9 %all-gather.6.cloned.1.call-start = ((), (), s32[]{:S(2)}) async-start(), calls=%async_computation.5 | async-start | bytes 2119680 | tf_op jit(solution)/shard_map/all_gather | solution.py:149
  443.8 7.9 %copy-start.6 = (bf16[1,2880,180]{1,2,0:T(8,128)(2,1)S(1)}, bf16[1,2880,180]{1,2,0:T(8,128)(2,1)}, u32[]{:S(2)}) copy-start(bf16[1,2880,180]{1,2,0:T(8,128)(2,1)} %param.28) | copy-start | bytes 3110404
  519.6 60.9 %all-to-all-start.2 = ((bf16[64,10,360]{2,1,0:T(8,128)(2,1)}), bf16[64,10,360]{2,1,0:T(8,128)(2,1)S(1)}, u32[]{:S(2)}, u32[]{:S(2)}) async-start(bf16[64,10,360]{2,1,0:T(8,128)(2,1)} %reshape.387), calls=%async_computation.2 | async-start | bytes 1572864 | tf_op jit(solution)/shard_map/all_to_all | solution.py:154
  535.8 2.5 copy-start.4
Sparse Core Ops, SparseCore 0:
  49.4 79.3 all-reduce.2
  195.7 231.1 all-gather.3
  457.0 55.4 all-gather.5
where the time goes:
time: 592 us; the launch traced here: 591 us
  waiting for transfers between devices  419 us (71%)
  blocking collectives  59.9 us (10%)
  local copies, waits for them, and re-layouts  45.1 us (8%)
  starting transfers between devices  35.2 us (6%)
  between operations  14.2 us (2%)
  matrix products  8.63 us (1%)
  other arithmetic  8.61 us (1%)
    all_gather x1, waiting for transfers between devices, on_device(): lax.all_gather(lax.all_to_all(outgoing, 'group', split_axis=0, concat_axi...  231 us
    psum x1, waiting for transfers between devices, on_device(): hidden_state = lax.psum(partial_sum, 'tp')  78.5 us
    all_to_all x1, blocking collectives, on_device(): lax.all_to_all(outgoing, 'group', split_axis=0, concat_axis=0, tiled=True)  59.9 us
    all_gather x1, waiting for transfers between devices, on_device(): joined = lax.all_gather(active, 'tp', axis=1, tiled=True)  55.6 us
    all_to_all x1, waiting for transfers between devices, on_device(): lax.all_to_all(returned, 'group', split_axis=0, concat_axis=0, tiled=True)  42 us
    all_to_all x1, starting transfers between devices, on_device(): lax.all_to_all(remote_pool.reshape(groups, -1, lane_count), 'group', spli...  18.9 us
    all_gather x1, local copies, waits for them, and re-layouts, on_device(): lax.all_gather(lax.all_to_all(outgoing, 'group', split_axis=0, concat_axi...  17 us
    all_to_all x1, starting transfers between devices, on_device(): lax.all_to_all(returned, 'group', split_axis=0, concat_axis=0, tiled=True)  16 us
  transfers between devices with their start and end apart: 5, of which 5 were waited for; matrix products, arithmetic and copies ran while one was open for 2% of the time, Pallas kernels for 0%

commit v1 on v0

--- a/solution.py
+++ b/solution.py
@@ -146,7 +146,9 @@
     gate_val = both[:, :hidden_part]
     up_val = both[:, hidden_part:]
     active = (gate_val * jax.nn.sigmoid(ALPHA * gate_val) * (up_val + 1.0)).astype(jnp.bfloat16)
-    joined = lax.all_gather(active, "tp", axis=1, tiled=True)
+    joined = jnp.concatenate(
+        lax.all_to_all(jnp.stack([active] * lax.axis_size("tp")), "tp", 0, 0), axis=1
+    )
     result = jnp.dot(joined, expert_down[0], preferred_element_type=jnp.float32).astype(
         jnp.bfloat16
     )

time: 592 us -> 562 us (0.949)
  the two profiles are of different devices: /device:TPU:2 before, /device:TPU:16 now
where the time goes in v1:
time: 562 us; the launch traced here: 561 us
  waiting for transfers between devices  362 us (64%)
  blocking collectives  89.7 us (16%)
  local copies, waits for them, and re-layouts  43.8 us (8%)
  starting transfers between devices  34.5 us (6%)
  between operations  14.5 us (3%)
  matrix products  8.4 us (1%)
  other arithmetic  7.92 us (1%)
    all_gather x1, waiting for transfers between devices, on_device(): lax.all_gather(lax.all_to_all(outgoing, 'group', split_axis=0, concat_axi...  229 us
    psum x1, waiting for transfers between devices, on_device(): hidden_state = lax.psum(partial_sum, 'tp')  81.7 us
    all_to_all x1, blocking collectives, on_device(): lax.all_to_all(outgoing, 'group', split_axis=0, concat_axis=0, tiled=True)  60.3 us
    all_to_all x1, waiting for transfers between devices, on_device(): lax.all_to_all(returned, 'group', split_axis=0, concat_axis=0, tiled=True)  42 us
    all_to_all x1, blocking collectives, on_device(): lax.all_to_all(jnp.stack([active] * lax.axis_size('tp')), 'tp', 0, 0)  29.3 us
    all_to_all x1, starting transfers between devices, on_device(): lax.all_to_all(remote_pool.reshape(groups, -1, lane_count), 'group', spli...  18.7 us
    all_gather x1, local copies, waits for them, and re-layouts, on_device(): lax.all_gather(lax.all_to_all(outgoing, 'group', split_axis=0, concat_axi...  17 us
    all_to_all x1, starting transfers between devices, on_device(): lax.all_to_all(returned, 'group', split_axis=0, concat_axis=0, tiled=True)  15.7 us
  transfers between devices with their start and end apart: 4, of which 4 were waited for; matrix products, arithmetic and copies ran while one was open for 2% of the time, Pallas kernels for 0%

profile of v1, /device:TPU:16, one launch (start us, length us, event | category | flops | bytes accessed | tf_op | source)
XLA Modules:
  0.0 561.2 jit_solution(2948831054669259254)
XLA Ops:
  6.5 18.7 %all-to-all-start = ((bf16[64,8,128]{2,1,0:T(8,128)(2,1)}), bf16[64,8,128]{2,1,0:T(8,128)(2,1)S(1)}, u32[]{:S(2)}, u32[]{:S(2)}) async-start(bf16[64,8,128]{2,1,0:T(8,128)(2,1)} %bitcast.65), calls=%async_computation | async-start | bytes 262144 | tf_op jit(solution)/shard_map/all_to_all | solution.py:87
  26.0 0.9 reshape.400
  26.9 0.8 copy.148
  27.8 0.9 copy.145
  28.8 0.7 add_bitcast_fusion
  29.7 0.2 broadcast_in_dim.31
  29.9 0.3 reshape.385
  30.2 0.3 copy.149
  30.7 0.1 fusion.30
  31.1 0.8 dynamic_slice.11
  31.9 0.2 multiply_cosine_fusion
  32.1 0.2 subtract_convert_fusion
  32.3 9.6 %all-to-all-done = bf16[64,8,128]{2,1,0:T(8,128)(2,1)S(1)} async-done(((bf16[64,8,128]{2,1,0:T(8,128)(2,1)}), bf16[64,8,128]{2,1,0:T(8,128)(2,1)S(1)}, u32[]{:S(2)}, u32[]{:S(2)}) %all-to-all-start) | async-done | bytes 131104 | tf_op jit(solution)/shard_map/all_to_all | solution.py:87
  42.1 0.7 slice_maximum_fusion
  42.8 0.3 copy.147
  43.1 0.4 fusion.39
  43.5 0.2 fusion.8
  43.7 0.3 copy.150
  44.0 0.3 fusion.5
  44.5 0.6 fusion.40
  45.2 0.9 dynamic_update_slice.3
  46.1 0.9 copy-done.1
  47.2 0.4 select_reduce_fusion
  48.0 81.7 %all-reduce.3.cloned.1.call-done = f32[64,2880]{1,0:T(8,128)} async-done(((f32[64,2880]{1,0:T(8,128)}), f32[64,2880]{1,0:T(8,128)}) %all-reduce.3.cloned.1.call-update) | async-done | bytes 737296 | tf_op jit(solution)/shard_map/psum | solution.py:109
  129.7 1.3 multiply_reduce_fusion
  131.0 1.0 multiply_convert_fusion
  132.0 2.0 gather_fusion
  134.2 0.2 select_multiply_fusion
  134.5 60.3 %all_to_all.20 = bf16[64,10,360]{2,1,0:T(8,128)(2,1)S(1)} all-to-all(bf16[64,10,360]{2,1,0:T(8,128)(2,1)S(1)} %bitcast.58), channel_id=1, replica_groups=mesh['group'=64,'tp'=8] {'group'}, dimensions={0} | all-to-all | bytes 921600 | tf_op jit(solution)/shard_map/all_to_all | solution.py:138
  194.8 2.0 copy.166
  196.8 229.1 %all-gather.2.cloned.1.call-done = bf16[64,10,2880]{0,1,2:T(8,128)(2,1)} async-done(((bf16[64,10,360]{0,1,2:T(8,128)(2,1)}), bf16[64,10,2880]{0,1,2:T(8,128)(2,1)}) %all-gather.2.cloned.1.call-update) | async-done | bytes 3686416 | tf_op jit(solution)/shard_map/all_gather | solution.py:137
  425.9 17.0 %copy.167 = bf16[64,10,2880]{2,1,0:T(8,128)(2,1)} copy(bf16[64,10,2880]{0,1,2:T(8,128)(2,1)} %all-gather.2.cloned.1.call-done) | data formatting | bytes 7372800 | tf_op jit(solution)/shard_map/all_gather | solution.py:137
  442.9 7.9 %reshape.394 = bf16[640,2880]{1,0:T(8,128)(2,1)} reshape(bf16[64,10,2880]{2,1,0:T(8,128)(2,1)} %copy.167) | data formatting | bytes 7372800 | tf_op jit(solution)/shard_map/reshape | solution.py:144
  450.7 4.3 fusion
  455.0 0.2 fusion.11
  455.2 0.1 stack.2
  455.4 29.3 %all_to_all.21 = bf16[8,640,180]{1,2,0:T(8,128)(2,1)S(1)} all-to-all(bf16[8,640,180]{1,2,0:T(8,128)(2,1)S(1)} %stack.2), channel_id=1, replica_groups=mesh['group'=64,'tp'=8] {'tp'}, dimensions={0} | all-to-all | bytes 3686400 | tf_op jit(solution)/shard_map/all_to_all | solution.py:150
  484.7 1.4 reshape.396
  486.1 2.9 convolution_convert_fusion
  489.0 0.3 copy.168
  489.3 1.1 reshape.397
  490.4 15.7 %all-to-all-start.3 = ((bf16[64,10,360]{2,1,0:T(8,128)(2,1)}), bf16[64,10,360]{2,1,0:T(8,128)(2,1)S(1)}, u32[]{:S(2)}, u32[]{:S(2)}) async-start(bf16[64,10,360]{2,1,0:T(8,128)(2,1)} %reshape.397), calls=%async_computation.3 | async-start | bytes 1572864 | tf_op jit(solution)/shard_map/all_to_all | solution.py:156
  506.3 1.9 gather_fusion.2
  509.0 42.0 %all-to-all-done.3 = bf16[64,10,360]{2,1,0:T(8,128)(2,1)S(1)} async-done(((bf16[64,10,360]{2,1,0:T(8,128)(2,1)}), bf16[64,10,360]{2,1,0:T(8,128)(2,1)S(1)}, u32[]{:S(2)}, u32[]{:S(2)}) %all-to-all-start.3) | async-done | bytes 460832 | tf_op jit(solution)/shard_map/all_to_all | solution.py:156
  550.9 0.2 convert.22
  551.3 1.0 gather_fusion.1
  552.4 0.4 multiply_reduce_fusion.1
  552.8 1.6 add_convert_fusion.1
  (69 shorter events, 3.2 us)
Async XLA Ops:
  6.5 38.0 %copy-start = (bf16[256,2880]{0,1:T(8,128)(2,1)S(1)}, bf16[256,2880]{0,1:T(8,128)(2,1)}, u32[]{:S(2)}) copy-start(bf16[256,2880]{0,1:T(8,128)(2,1)} %param.22) | copy-start | bytes 4423684
  6.5 24.0 %copy-start.5 = (f32[4]{0:T(128)S(1)}, f32[4]{0:T(128)}, u32[]{:S(2)}) copy-start(f32[4]{0:T(128)} %param.21) | copy-start | bytes 52
  6.5 24.3 %copy-start.3 = (s32[64,4]{0,1:T(4,128)S(1)}, s32[64,4]{0,1:T(4,128)}, u32[]{:S(2)}) copy-start(s32[64,4]{0,1:T(4,128)} %param.25) | copy-start | bytes 3076
  6.5 35.4 %all-to-all-start = ((bf16[64,8,128]{2,1,0:T(8,128)(2,1)}), bf16[64,8,128]{2,1,0:T(8,128)(2,1)S(1)}, u32[]{:S(2)}, u32[]{:S(2)}) async-start(bf16[64,8,128]{2,1,0:T(8,128)(2,1)} %bitcast.65), calls=%async_computation | async-start | bytes 262144 | tf_op jit(solution)/shard_map/all_to_all | solution.py:87
  25.3 104.4 %all-reduce.3.cloned.1.call-start = ((), (), s32[]{:S(2)}) async-start(), calls=%async_computation.4 | async-start | bytes 1507328 | tf_op jit(solution)/shard_map/psum | solution.py:109
  44.0 1.1 copy-start.2
  46.1 0.9 copy-start.1
  47.0 378.9 %all-gather.2.cloned.1.call-start = ((), (), s32[]{:S(2)}) async-start(), calls=%async_computation.5 | async-start | bytes 13271040 | tf_op jit(solution)/shard_map/all_gather | solution.py:137
  442.9 7.9 %copy-start.6 = (bf16[1,2880,180]{1,2,0:T(8,128)(2,1)S(1)}, bf16[1,2880,180]{1,2,0:T(8,128)(2,1)}, u32[]{:S(2)}) copy-start(bf16[1,2880,180]{1,2,0:T(8,128)(2,1)} %param.28) | copy-start | bytes 3110404
  490.4 60.5 %all-to-all-start.3 = ((bf16[64,10,360]{2,1,0:T(8,128)(2,1)}), bf16[64,10,360]{2,1,0:T(8,128)(2,1)S(1)}, u32[]{:S(2)}, u32[]{:S(2)}) async-start(bf16[64,10,360]{2,1,0:T(8,128)(2,1)} %reshape.397), calls=%async_computation.3 | async-start | bytes 1572864 | tf_op jit(solution)/shard_map/all_to_all | solution.py:156
  506.3 2.5 copy-start.4
Sparse Core Ops, SparseCore 0:
  47.1 82.5 all-reduce.2
  196.9 228.9 all-gather.1
